TPU v7x, 32 devices: a whole 2x2x4 slice. The times are simulated.
32 devices in a mesh: grp: 2 (over y), wide: 4 (over z), freq: 2 (over x), pol: 2 (over core).
Axes of the slice: x: 2, y: 2, z: 4, core: 2. Of those that a mesh axis runs over, the one named last changes fastest.
Arguments:
- visibilities: float32 [2, 4096, 8, 384], P(None, ('grp', 'wide'), 'freq', 'pol'), parts along dimension 1, may hold values from -6 to 6
- beams: bfloat16 [8, 8, 2, 384, 768], P('wide', 'freq', None, 'pol'), may hold values from -0.21875 to 0.21875
- spectra: float32 [8, 5, 768], P('freq'), may hold values from 0.1 to 1
- m_orders: int32 [8], replicated, may hold values from 0 to 1023, as said below
Outputs:
- msdata: float32 [16, 8, 2, 384], P(('grp', 'wide'), 'freq', None, 'pol'), parts along dimension 0
- weighted: float32 [16, 8, 2, 384], P(('grp', 'wide'), 'freq', None, 'pol'), parts along dimension 0
There are 2 independent parts, one for each index of `grp`. A program takes and returns all parts, laid end to end along the dimension named above; an argument that names none is the same for every part. Nothing has to cross between parts.
Inputs may be any that keep to these rules, and one draw needn't show every extreme that they name: `m_orders`: the m-orders are distinct, and 0 and 1023 are always among them.
All inputs are finite; a program needn't handle non-finite values.
Results may differ from a plain program's by a relative error of at most 0.0039.
Values sent between devices are 32-bit elements; how exact they have to be, the bound alone decides.
A program may use at most 64 MiB of HBM per device.

v0:
```python
import math

import jax
import jax.numpy as jnp
from jax import lax
from jax.sharding import PartitionSpec as P

TIME = 2048
BAND = 4


def shifted(array, axis, by):
    size = lax.axis_size(axis)
    return lax.ppermute(array, axis, [(i, (i + by) % size) for i in range(size)])


def fourier_tables(orders, times):
    product = orders[:, None] * times[None, :] % TIME
    angle = product.astype(jnp.float32) * (2.0 * math.pi / TIME)
    factor = 1.0 / math.sqrt(TIME)
    return (jnp.cos(angle) * factor, jnp.sin(angle) * factor)


def transform(orders, times, block):
    cosine, sine_tab = fourier_tables(orders, times)
    count = times.shape[0]
    data_real = block[0].reshape(count, -1)
    data_imag = block[1].reshape(count, -1)
    exact_mode = lax.Precision.HIGHEST
    part_real = jnp.dot(
        cosine, data_real, precision=exact_mode, preferred_element_type=jnp.float32
    ) + jnp.dot(sine_tab, data_imag, precision=exact_mode, preferred_element_type=jnp.float32)
    part_imag = jnp.dot(
        cosine, data_imag, precision=exact_mode, preferred_element_type=jnp.float32
    ) - jnp.dot(sine_tab, data_real, precision=exact_mode, preferred_element_type=jnp.float32)
    shape_out = (orders.shape[0], block.shape[2], block.shape[3])
    return jnp.stack([part_real.reshape(shape_out), part_imag.reshape(shape_out)], axis=2)


def shards(visibilities, beams, spectra, m_orders):
    local_blocks = beams.shape[1]
    local_times = visibilities.shape[1]
    first_time = lax.axis_index("wide") * local_times
    times = first_time + jnp.arange(local_times, dtype=jnp.int32)
    msdata = lax.psum_scatter(
        transform(m_orders, times, visibilities), "wide", scatter_dimension=0, tiled=True
    )
    rounded = msdata.astype(jnp.bfloat16)
    round_real = rounded[:, :, 0]
    round_imag = rounded[:, :, 1]
    stacked = jnp.stack(
        [jnp.stack([round_real, round_imag], 2), jnp.stack([round_imag, -round_real], 2)], 2
    )
    partial_proj = lax.dot_general(
        stacked, beams, (((3, 4), (2, 3)), ((0, 1), (0, 1))), preferred_element_type=jnp.float32
    )
    projected = lax.psum(partial_proj, "pol")
    following = shifted(projected, "freq", -1)
    extended = jnp.concatenate([projected, following], axis=1)
    mixed = spectra[None, :, 0, None, :] * projected
    for offset in range(1, BAND + 1):
        mixed = (
            mixed + spectra[None, :, offset, None, :] * extended[:, offset : offset + local_blocks]
        )
    coupled = mixed.astype(jnp.bfloat16)
    cop_real = coupled[:, :, 0]
    cop_imag = coupled[:, :, 1]
    paired = jnp.stack([jnp.stack([cop_real, -cop_imag], 2), jnp.stack([cop_imag, cop_real], 2)], 2)
    weighted = lax.dot_general(
        paired, beams, (((3, 4), (2, 4)), ((0, 1), (0, 1))), preferred_element_type=jnp.float32
    )
    return (msdata, weighted)


def solution(mesh):
    return jax.shard_map(
        shards,
        mesh=mesh,
        in_specs=(
            P(None, ("grp", "wide"), "freq", "pol"),
            P("wide", "freq", None, "pol", None),
            P("freq", None, None),
            P(),
        ),
        out_specs=(
            P(("grp", "wide"), "freq", None, "pol"),
            P(("grp", "wide"), "freq", None, "pol"),
        ),
        check_vma=False,
    )
```

profile of v0, /device:TPU:0, one launch (start us, length us, event | category | flops | bytes accessed | tf_op | source)
XLA Modules:
  0.0 47.3 jit_solution(1263961565827750037)
XLA Ops:
  0.6 0.0 copy-start.1
  0.7 2.2 %fusion.44 = (f32[1,512,4,192]{1,3,2,0:T(8,128)S(1)}, f32[1,512,4,192]{1,3,2,0:T(8,128)S(1)}) fusion(f32[2,512,4,192]{1,3,2,0:T(8,128)} %param.4), kind=kLoop, calls=%fused_computation.70 | loop fusion | bytes 6291456 | tf_op jit(solution)/shard_map/slice | solution.py:27
  2.9 0.0 copy-done.1
  2.9 1.4 %fusion.13 = f32[8,768]{1,0:T(8,128)S(1)} fusion(f32[512,768]{0,1:T(8,128)S(1)} %bitcast.34, s32[512]{0:T(512)S(1)} %iota_add_fusion, s32[8]{0:T(128)S(1)} %copy-done.1), kind=kOutput, calls=%fused_computation.31 | convolution fusion | flops 37810176 | bytes 1599520 | tf_op jit(solution)/shard_map/dot_general | solution.py:30
  4.3 1.5 %fusion.12 = f32[8,768]{1,0:T(8,128)S(1)} fusion(f32[512,768]{0,1:T(8,128)S(1)} %bitcast.36, s32[512]{0:T(512)S(1)} %iota_add_fusion, s32[8]{0:T(128)S(1)} %copy-done.1), kind=kOutput, calls=%fused_computation.30 | convolution fusion | flops 37810176 | bytes 1599520 | tf_op jit(solution)/shard_map/dot_general | solution.py:33
  5.8 0.0 copy-start.2
  5.8 1.5 %convolution_add_fusion = f32[8,768]{1,0:T(8,128)S(1)} fusion(f32[8,768]{1,0:T(8,128)S(1)} %fusion.13, f32[512,768]{0,1:T(8,128)S(1)} %bitcast.37, s32[512]{0:T(512)S(1)} %iota_add_fusion, s32[8]{0:T(128)S(1)} %copy-done.1), kind=kOutput, calls=%fused_computation.2 | convolution fusion | flops 37816320 | bytes 1624096 | tf_op jit(solution)/shard_map/dot_general | solution.py:32
  7.3 0.1 stack_reshape.6
  7.4 1.4 %convolution_subtract_fusion = f32[8,768]{1,0:T(8,128)S(1)} fusion(f32[8,768]{1,0:T(8,128)S(1)} %fusion.12, f32[512,768]{0,1:T(8,128)S(1)} %bitcast.35, s32[512]{0:T(512)S(1)} %iota_add_fusion, s32[8]{0:T(128)S(1)} %copy-done.1), kind=kOutput, calls=%fused_computation.1 | convolution fusion | flops 37816320 | bytes 1624096 | tf_op jit(solution)/shard_map/dot_general | solution.py:35
  8.8 0.1 stack_reshape.7
  9.0 21.5 %all-reduce = f32[8,4,2,192]{3,1,2,0:T(4,128)S(1)} all-reduce(f32[8,4,2,192]{3,1,2,0:T(4,128)S(1)} %pad_maximum_fusion), channel_id=2, replica_groups=mesh['grp'=2,'wide'=4,'freq'=2,'pol'=2] {'wide'}, use_global_device_ids=true, to_apply=%region_0.1.clone | all-reduce | flops 12288 | bytes 98304
  30.5 0.0 copy-done.2
  30.5 0.6 %dynamic-slice = u32[1]{0:T(128)} dynamic-slice(u32[32]{0:T(128)S(1)} %copy-done.2, u32[]{:T(128)S(6)} %add.44), dynamic_slice_sizes={1} | dynamic-slice | bytes 12
  31.9 0.0 copy-start
  31.9 3.1 %convolution_bitcast_fusion = f32[2,4,2,768]{3,2,1,0:T(2,128)S(1)} fusion(bf16[2,4,2,192,768]{4,3,2,1,0:T(8,128)(2,1)} %param.5, bf16[2,4,1,2,192]{4,2,3,1,0:T(2,128)(2,1)S(1)} %copy.24, bf16[2,4,1,2,192]{4,2,3,1,0:T(2,128)(2,1)S(1)} %copy.23), kind=kOutput, calls=%fused_computation | convolution fusion | flops 9461760 | bytes 4780032 | tf_op jit(solution)/shard_map/dot_general | solution.py:54
  35.0 3.5 %psum.7 = f32[2,4,2,768]{3,2,1,0:T(2,128)S(1)} all-reduce(f32[2,4,2,768]{3,2,1,0:T(2,128)S(1)} %convolution_bitcast_fusion), channel_id=1, replica_groups=mesh['grp'=2,'wide'=4,'freq'=2,'pol'=2] {'pol'}, use_global_device_ids=true, to_apply=%region_1.2 | all-reduce | flops 12288 | bytes 98304 | tf_op jit(solution)/shard_map/psum | solution.py:57
  38.5 1.6 %collective-permute-start = (f32[2,4,2,768]{3,2,1,0:T(2,128)S(1)}, f32[2,4,2,768]{3,2,1,0:T(2,128)S(1)}, u32[]{:S(2)}, u32[]{:S(2)}) collective-permute-start(f32[2,4,2,768]{3,2,1,0:T(2,128)S(1)} %psum.7), channel_id=1, source_target_pairs={{0,2},{2,0},{1,3},{3,1},{4,6},{6,4},{5,7},{7,5},{8,10},{10,8},{9,1... | collective-permute-start | bytes 147464 | tf_op jit(solution)/shard_map/ppermute | solution.py:14
  40.1 0.0 copy-done
  40.1 0.6 %copy.26 = f32[2,4,2,192]{3,2,1,0:T(2,128)} copy(f32[2,4,2,192]{3,1,2,0:T(4,128)S(1)} %get-tuple-element.5) | data formatting | bytes 24576
  40.7 2.0 %collective-permute-done = f32[2,4,2,768]{3,2,1,0:T(2,128)S(1)} collective-permute-done((f32[2,4,2,768]{3,2,1,0:T(2,128)S(1)}, f32[2,4,2,768]{3,2,1,0:T(2,128)S(1)}, u32[]{:S(2)}, u32[]{:S(2)}) %collective-permute-start) | collective-permute-done | bytes 49184 | tf_op jit(solution)/shard_map/ppermute | solution.py:14
  42.7 0.1 fusion.5
  42.8 0.1 slice_negate_fusion.1
  42.9 0.1 maximum_bitcast_fusion
  43.0 0.1 pad_maximum_fusion.1
  43.1 4.3 %convolution_bitcast_fusion.1 = f32[2,4,2,192]{3,2,1,0:T(2,128)} fusion(bf16[2,4,2,192,768]{4,3,2,1,0:T(8,128)(2,1)} %param.5, bf16[2,4,2,2,768]{4,3,1,0,2:T(2,128)(2,1)S(1)} %pad_maximum_fusion.1), kind=kOutput, calls=%fused_computation.3 | convolution fusion | flops 9437184 | bytes 4780032 | tf_op jit(solution)/shard_map/dot_general | solution.py:69
  (10 shorter events, 0.1 us)
Async XLA Ops:
  0.6 2.2 %copy-start.1 = (s32[8]{0:T(128)S(1)}, s32[8]{0:T(128)}, u32[]{:S(2)}) copy-start(s32[8]{0:T(128)} %param.7) | copy-start | bytes 100
  5.8 24.7 %copy-start.2 = (u32[32]{0:T(128)S(1)}, u32[32]{0:T(128)}, u32[]{:S(2)}) copy-start(u32[32]{0:T(128)} %constant.29) | copy-start | bytes 388
  31.9 8.2 %copy-start = (f32[4,5,768]{2,0,1:T(4,128)S(1)}, f32[4,5,768]{2,0,1:T(4,128)}, u32[]{:S(2)}) copy-start(f32[4,5,768]{2,0,1:T(4,128)} %param.6) | copy-start | bytes 184324
  38.5 4.2 %collective-permute-start = (f32[2,4,2,768]{3,2,1,0:T(2,128)S(1)}, f32[2,4,2,768]{3,2,1,0:T(2,128)S(1)}, u32[]{:S(2)}, u32[]{:S(2)}) collective-permute-start(f32[2,4,2,768]{3,2,1,0:T(2,128)S(1)} %psum.7), channel_id=1, source_target_pairs={{0,2},{2,0},{1,3},{3,1},{4,6},{6,4},{5,7},{7,5},{8,10},{10,8},{9,1... | collective-permute-start | bytes 147464 | tf_op jit(solution)/shard_map/ppermute | solution.py:14
where the time goes:
time: 47.6 us; the launch traced here: 47.3 us
  blocking collectives  25 us (53%)
  matrix products  13.3 us (28%)
  local copies, waits for them, and re-layouts  3.68 us (8%)
  waiting for transfers between devices  1.96 us (4%)
  starting transfers between devices  1.56 us (3%)
  between operations  1.46 us (3%)
    unnamed x1, blocking collectives  21.5 us
    dot_general x1, matrix products, shards(): lax.dot_general(paired, beams, (((3, 4), (2, 4)), ((0, 1), (0, 1))), pref...  4.27 us
    psum x1, blocking collectives, shards(): projected = lax.psum(partial_proj, 'pol')  3.52 us
    dot_general x1, matrix products, shards(): lax.dot_general(stacked, beams, (((3, 4), (2, 3)), ((0, 1), (0, 1))), pre...  3.14 us
    slice x1, local copies, waits for them, and re-layouts, transform(): data_real = block[0].reshape(count, -1)  2.19 us
    ppermute x1, waiting for transfers between devices, shifted(): lax.ppermute(array, axis, [(i, (i + by) % size) for i in range(size)])  1.96 us
    ppermute x1, starting transfers between devices, shifted(): lax.ppermute(array, axis, [(i, (i + by) % size) for i in range(size)])  1.56 us
    dot_general x1, matrix products, transform(): jnp.dot(cosine, data_imag, precision=exact_mode, preferred_element_type=j...  1.48 us
  transfers between devices with their start and end apart: 1, of which 1 were waited for; matrix products, arithmetic and copies ran while one was open for 1% of the time, Pallas kernels for 0%

commit v1 on v0

v1 whole, which is shorter than its diff:
```python
import functools
import math

import jax
import jax.numpy as jnp
from jax import lax
from jax.experimental import pallas as pl
from jax.experimental.pallas import tpu as pltpu
from jax.sharding import PartitionSpec as P

TIME = 2048
QUARTER = TIME // 4
BAND = 4
PIECES = 2
MESH = pl.DeviceIdType.MESH
NT = (((1,), (1,)), ((), ()))
NN = (((1,), (0,)), ((), ()))


def cosine(steps):
    near = steps + QUARTER // 2
    quadrant = (near // QUARTER) & 3
    x = ((near & (QUARTER - 1)) - QUARTER // 2).astype(jnp.float32) * (2.0 * math.pi / TIME)
    y = x * x
    cos = 1.0 + y * (-1 / 2 + y * (1 / 24 + y * (-1 / 720 + y * (1 / 40320))))
    sin = x * (1.0 + y * (-1 / 6 + y * (1 / 120 + y * (-1 / 5040 + y * (1 / 362880)))))
    value = jnp.where((quadrant & 1) == 1, sin, cos)
    return jnp.where((quadrant == 1) | (quadrant == 2), -value, value)


def high_low(array):
    high = array.astype(jnp.bfloat16)
    return high, (array - high.astype(jnp.float32)).astype(jnp.bfloat16)


def turned(array, sign):
    rows = []
    for order in range(array.shape[0] // 2):
        real, imag = array[2 * order : 2 * order + 1], array[2 * order + 1 : 2 * order + 2]
        rows += [imag, -real] if sign > 0 else [-imag, real]
    return jnp.concatenate(rows, axis=0)


def kernel(
    wide, freq, orders_hbm, vis_hbm, beams_hbm, spectra_hbm, ms_ref, out_ref,
    orders, vis, beams, spectra, part, recv, proj, recv_proj,
    order_sem, vis_sem, beam_sem, spectra_sem, send_sem, recv_sem, psend_sem, precv_sem,
):
    my_wide, my_freq, my_pol = lax.axis_index("wide"), lax.axis_index("freq"), lax.axis_index("pol")
    _, blocks, modes, times = vis.shape
    total, local = orders.shape[0], ms_ref.shape[0]
    rows = 2 * local

    order_copy = pltpu.make_async_copy(orders_hbm, orders, order_sem)
    order_copy.start()
    vis_copies = [
        pltpu.make_async_copy(vis_hbm.at[:, f], vis.at[:, f], vis_sem.at[f]) for f in range(blocks)
    ]
    for copy in vis_copies:
        copy.start()
    before = lax.rem(my_freq + freq - 1, freq)
    after = lax.rem(my_freq + 1, freq)
    barrier = pltpu.get_barrier_semaphore()
    greeted = [{"wide": lax.rem(my_wide + j, wide)} for j in range(1, wide)]
    greeted += [{"pol": 1 - my_pol}, {"freq": before}, {"freq": before, "pol": 1 - my_pol}]
    if freq > 2:
        greeted += [{"freq": after}, {"freq": after, "pol": 1 - my_pol}]
    for device in greeted:
        pl.semaphore_signal(barrier, inc=1, device_id=device, device_id_type=MESH)
    beam_copies = [
        pltpu.make_async_copy(beams_hbm.at[:, f], beams.at[:, f], beam_sem.at[f])
        for f in range(blocks)
    ]
    for copy in beam_copies:
        copy.start()
    spectra_copy = pltpu.make_async_copy(spectra_hbm, spectra, spectra_sem)
    spectra_copy.start()

    shape = (2 * total, times)
    row = lax.broadcasted_iota(jnp.int32, shape, 0)
    time = lax.broadcasted_iota(jnp.int32, shape, 1) + my_wide * times
    order_copy.wait()
    order = jnp.zeros(shape, jnp.int32)
    for i in range(total):
        order = jnp.where(row // 2 == i, orders[i], order)
    steps = order * time
    imag_row = (row & 1) == 1
    factor = 1.0 / math.sqrt(TIME)
    stacks, highs = [], []
    for shift in (jnp.where(imag_row, QUARTER, 0), jnp.where(imag_row, 0, 3 * QUARTER)):
        high, low = high_low(cosine(steps + shift) * factor)
        stacks.append(jnp.concatenate([high, low], axis=0))
        highs.append(high)

    for f in range(blocks):
        vis_copies[f].wait()
        both = jnp.zeros((4 * total, modes), jnp.float32)
        small = jnp.zeros((2 * total, modes), jnp.float32)
        for c in range(2):
            high, low = high_low(vis[c, f])
            both += lax.dot_general(stacks[c], high, NT, preferred_element_type=jnp.float32)
            small += lax.dot_general(highs[c], low, NT, preferred_element_type=jnp.float32)
        result = both[: 2 * total] + (both[2 * total :] + small)
        for w in range(wide):
            part[w, f] = result[rows * w : rows * (w + 1)]

    pl.semaphore_wait(barrier, len(greeted))
    sends = []
    for j in range(1, wide):
        target = lax.rem(my_wide + j, wide)
        copy = pltpu.make_async_remote_copy(
            src_ref=part.at[target],
            dst_ref=recv.at[j - 1],
            send_sem=send_sem.at[j - 1],
            recv_sem=recv_sem.at[j - 1],
            device_id={"wide": target},
            device_id_type=MESH,
        )
        copy.start()
        sends.append(copy)
    for copy in sends:
        copy.wait_recv()

    order_of_row = lax.broadcasted_iota(jnp.int32, (rows, modes), 0) // 2
    targets = [{"pol": 1 - my_pol}, {"freq": before}, {"freq": before, "pol": 1 - my_pol}]
    piece = blocks // PIECES
    proj_sends = []
    for f in range(blocks):
        summed = part[my_wide, f]
        for j in range(wide - 1):
            summed += recv[j, f]
        for o in range(local):
            ms_ref[o, f] = summed[2 * o : 2 * o + 2]
        other = turned(summed, 1)
        beam_copies[f].wait()
        acc = jnp.zeros((rows, beams.shape[-1]), jnp.float32)
        for o in range(local):
            mine = order_of_row == o
            for c, data in ((0, summed), (1, other)):
                left = jnp.where(mine, data, 0.0).astype(jnp.bfloat16)
                acc += lax.dot_general(
                    left, beams[o, f, c], NN, preferred_element_type=jnp.float32
                )
        proj[f] = acc
        if f % piece == piece - 1:
            g = f // piece
            span = pl.ds(g * piece, piece)
            for s, target in enumerate(targets):
                copy = pltpu.make_async_remote_copy(
                    src_ref=proj.at[span],
                    dst_ref=recv_proj.at[s, span],
                    send_sem=psend_sem.at[s, g],
                    recv_sem=precv_sem.at[s, g],
                    device_id=target,
                    device_id_type=MESH,
                )
                copy.start()
                proj_sends.append(copy)
    spectra_copy.wait()
    for copy in proj_sends:
        copy.wait_recv()

    extended = [proj[f] + recv_proj[0, f] for f in range(blocks)]
    extended += [recv_proj[1, f] + recv_proj[2, f] for f in range(blocks)]
    order_of_row = lax.broadcasted_iota(jnp.int32, (rows, beams.shape[-1]), 0) // 2
    for f in range(blocks):
        mixed = spectra[0, f : f + 1] * extended[f]
        for d in range(1, BAND + 1):
            mixed = mixed + spectra[d, f : f + 1] * extended[f + d]
        other = turned(mixed, -1)
        acc = jnp.zeros((rows, modes), jnp.float32)
        for o in range(local):
            mine = order_of_row == o
            for c, data in ((0, mixed), (1, other)):
                left = jnp.where(mine, data, 0.0).astype(jnp.bfloat16)
                acc += lax.dot_general(
                    left, beams[o, f, c], NT, preferred_element_type=jnp.float32
                )
        for o in range(local):
            out_ref[o, f] = acc[2 * o : 2 * o + 2]
    for copy in sends + proj_sends:
        copy.wait_send()


def shards(wide, freq, visibilities, beams, spectra, m_orders):
    local, blocks, _, modes, degrees = beams.shape
    times = visibilities.shape[1]
    rows = 2 * local
    result = jax.ShapeDtypeStruct((local, blocks, 2, modes), jnp.float32)
    dma = pltpu.SemaphoreType.DMA
    return pl.pallas_call(
        functools.partial(kernel, wide, freq),
        out_shape=(result, result),
        in_specs=[pl.BlockSpec(memory_space=pl.ANY)] * 4,
        out_specs=(pl.BlockSpec(memory_space=pltpu.VMEM),) * 2,
        scratch_shapes=[
            pltpu.SMEM(m_orders.shape, jnp.int32),
            pltpu.VMEM((2, blocks, modes, times), jnp.float32),
            pltpu.VMEM(beams.shape, beams.dtype),
            pltpu.VMEM((BAND + 1, blocks, degrees), jnp.float32),
            pltpu.VMEM((wide, blocks, rows, modes), jnp.float32),
            pltpu.VMEM((wide - 1, blocks, rows, modes), jnp.float32),
            pltpu.VMEM((blocks, rows, degrees), jnp.float32),
            pltpu.VMEM((3, blocks, rows, degrees), jnp.float32),
            dma,
            dma((blocks,)),
            dma((blocks,)),
            dma,
            dma((wide - 1,)),
            dma((wide - 1,)),
            dma((3, PIECES)),
            dma((3, PIECES)),
        ],
        compiler_params=pltpu.CompilerParams(
            collective_id=0, has_side_effects=True, vmem_limit_bytes=48 << 20
        ),
    )(
        m_orders,
        jnp.transpose(visibilities, (0, 2, 3, 1)),
        beams,
        jnp.transpose(spectra, (1, 0, 2)),
    )


def solution(mesh):
    return jax.shard_map(
        functools.partial(shards, mesh.shape["wide"], mesh.shape["freq"]),
        mesh=mesh,
        in_specs=(
            P(None, ("grp", "wide"), "freq", "pol"),
            P("wide", "freq", None, "pol", None),
            P("freq", None, None),
            P(),
        ),
        out_specs=(
            P(("grp", "wide"), "freq", None, "pol"),
            P(("grp", "wide"), "freq", None, "pol"),
        ),
        check_vma=False,
    )
```

time: 47.6 us -> 21.4 us (0.45)
  blocking collectives: 25 us -> 0 us
  Pallas kernels: 0 us -> 15.9 us
  matrix products: 13.3 us -> 0 us
  waiting for transfers between devices: 1.96 us -> 0 us
  starting transfers between devices: 1.56 us -> 0 us
  local copies, waits for them, and re-layouts: 3.68 us -> 4.58 us
  between operations: 1.46 us -> 0.65 us
    unnamed x1 -> x0, blocking collectives: 21.5 us -> none
    pallas_call x0 -> x1, Pallas kernels: none -> 15.9 us  [shards(): pl.pallas_call(functools.partial(kernel, wide, freq), out_shape=(result,...]
    dot_general x6 -> x0, matrix products: 13.3 us -> none  [the longest x1 4.27 us: shards(): lax.dot_general(paired, beams, (((3, 4), (2, 4)), ((0, 1), (0, 1))), pref...]
    psum x1 -> x0, blocking collectives: 3.52 us -> none  [shards(): projected = lax.psum(partial_proj, 'pol')]
    unnamed x9 -> x8, local copies, waits for them, and re-layouts: 1.22 us -> 4.58 us
    slice x1 -> x0, local copies, waits for them, and re-layouts: 2.19 us -> none  [transform(): data_real = block[0].reshape(count, -1)]
    ppermute x1 -> x0, waiting for transfers between devices: 1.96 us -> none  [shifted(): lax.ppermute(array, axis, [(i, (i + by) % size) for i in range(size)])]
    ppermute x1 -> x0, starting transfers between devices: 1.56 us -> none  [shifted(): lax.ppermute(array, axis, [(i, (i + by) % size) for i in range(size)])]
  transfers between devices with their start and end apart: 1 -> 0, of which waited for: 1 -> 0; matrix products, arithmetic and copies ran while one was open for 1% -> 0% of each run, Pallas kernels for 0% -> 0%
where the time goes in v1:
time: 21.4 us; the launch traced here: 21.2 us
  Pallas kernels  15.9 us (74%)
  local copies, waits for them, and re-layouts  4.58 us (21%)
  between operations  0.65 us (3%)
    pallas_call x1, Pallas kernels, shards(): pl.pallas_call(functools.partial(kernel, wide, freq), out_shape=(result,...  15.9 us
    unnamed x8, local copies, waits for them, and re-layouts  4.58 us

profile of v1, /device:TPU:0, one launch (start us, length us, event | category | flops | bytes accessed | tf_op | source)
XLA Modules:
  0.0 21.2 jit_solution(9198519375460738711)
XLA Ops:
  0.6 0.0 copy-start
  0.6 1.9 %copy-done = f32[2,512,4,192]{1,3,2,0:T(8,128)S(1)} copy-done((f32[2,512,4,192]{1,3,2,0:T(8,128)S(1)}, f32[2,512,4,192]{1,3,2,0:T(8,128)}, u32[]{:S(2)}) %copy-start) | copy-done | bytes 3145752
  2.5 0.0 copy-start.1
  2.5 0.8 %copy-done.1 = f32[4,5,768]{2,0,1:T(4,128)S(1)} copy-done((f32[4,5,768]{2,0,1:T(4,128)S(1)}, f32[4,5,768]{2,0,1:T(4,128)}, u32[]{:S(2)}) %copy-start.1) | copy-done | bytes 61464
  3.4 0.0 copy-start.2
  3.4 0.7 %copy-done.2 = s32[8]{0:T(128)S(1)} copy-done((s32[8]{0:T(128)S(1)}, s32[8]{0:T(128)}, u32[]{:S(2)}) %copy-start.2) | copy-done | bytes 56
  4.0 15.9 %shard_map.59 = (f32[2,4,2,192]{3,2,1,0:T(2,128)S(1)}, f32[2,4,2,192]{3,2,1,0:T(2,128)S(1)}) custom-call(s32[8]{0:T(128)S(1)} %copy-done.2, f32[2,4,192,512]{3,2,1,0:T(8,128)S(1)} %bitcast.2, bf16[2,4,2,192,768]{4,3,2,1,0:T(8,128)(2,1)} %beams_hbm.1, f32[5,4,768]{2,1,0:T(4,128)S(1)} %bitcast.3), custom_call_target="tpu_custom_call" | custom-call | tf_op jit(solution)/shard_map/pallas_call | solution.py:191
  19.9 0.6 %copy.8 = f32[2,4,2,192]{3,2,1,0:T(2,128)} copy(f32[2,4,2,192]{3,2,1,0:T(2,128)S(1)} %get-tuple-element.4) | data formatting | bytes 24576
  20.5 0.6 %copy.9 = f32[2,4,2,192]{3,2,1,0:T(2,128)} copy(f32[2,4,2,192]{3,2,1,0:T(2,128)S(1)} %get-tuple-element.5) | data formatting | bytes 24576
Async XLA Ops:
  0.6 1.9 %copy-start = (f32[2,512,4,192]{1,3,2,0:T(8,128)S(1)}, f32[2,512,4,192]{1,3,2,0:T(8,128)}, u32[]{:S(2)}) copy-start(f32[2,512,4,192]{1,3,2,0:T(8,128)} %param.4) | copy-start | bytes 9437188
  2.5 0.8 %copy-start.1 = (f32[4,5,768]{2,0,1:T(4,128)S(1)}, f32[4,5,768]{2,0,1:T(4,128)}, u32[]{:S(2)}) copy-start(f32[4,5,768]{2,0,1:T(4,128)} %param.6) | copy-start | bytes 184324
  3.4 0.7 %copy-start.2 = (s32[8]{0:T(128)S(1)}, s32[8]{0:T(128)}, u32[]{:S(2)}) copy-start(s32[8]{0:T(128)} %orders_hbm.1) | copy-start | bytes 100

commit v2 on v1

--- a/solution.py
+++ b/solution.py
@@ -42,11 +42,12 @@
 
 
 def kernel(
-    wide, freq, orders_hbm, vis_hbm, beams_hbm, spectra_hbm, ms_ref, out_ref,
+    wide, freq, orders_hbm, vis_hbm, beams_hbm, spectra_hbm, result_ref,
     orders, vis, beams, spectra, part, recv, proj, recv_proj,
     order_sem, vis_sem, beam_sem, spectra_sem, send_sem, recv_sem, psend_sem, precv_sem,
 ):
     my_wide, my_freq, my_pol = lax.axis_index("wide"), lax.axis_index("freq"), lax.axis_index("pol")
+    ms_ref, out_ref = result_ref.at[0], result_ref.at[1]
     _, blocks, modes, times = vis.shape
     total, local = orders.shape[0], ms_ref.shape[0]
     rows = 2 * local
@@ -186,13 +187,13 @@
     local, blocks, _, modes, degrees = beams.shape
     times = visibilities.shape[1]
     rows = 2 * local
-    result = jax.ShapeDtypeStruct((local, blocks, 2, modes), jnp.float32)
+    result = jax.ShapeDtypeStruct((2, local, blocks, 2, modes), jnp.float32)
     dma = pltpu.SemaphoreType.DMA
-    return pl.pallas_call(
+    both = pl.pallas_call(
         functools.partial(kernel, wide, freq),
-        out_shape=(result, result),
+        out_shape=result,
         in_specs=[pl.BlockSpec(memory_space=pl.ANY)] * 4,
-        out_specs=(pl.BlockSpec(memory_space=pltpu.VMEM),) * 2,
+        out_specs=pl.BlockSpec(memory_space=pltpu.VMEM),
         scratch_shapes=[
             pltpu.SMEM(m_orders.shape, jnp.int32),
             pltpu.VMEM((2, blocks, modes, times), jnp.float32),
@@ -212,7 +213,7 @@
             dma((3, PIECES)),
         ],
         compiler_params=pltpu.CompilerParams(
-            collective_id=0, has_side_effects=True, vmem_limit_bytes=48 << 20
+            collective_id=0, has_side_effects=True, vmem_limit_bytes=64 << 20
         ),
     )(
         m_orders,
@@ -220,6 +221,7 @@
         beams,
         jnp.transpose(spectra, (1, 0, 2)),
     )
+    return both[0], both[1]
 
 
 def solution(mesh):

time: 21.4 us -> 19.2 us (0.90)
  local copies, waits for them, and re-layouts: 4.58 us -> 1.35 us
  Pallas kernels: 15.9 us -> 17 us
    unnamed x8 -> x0, local copies, waits for them, and re-layouts: 4.58 us -> none
    squeeze x0 -> x1, local copies, waits for them, and re-layouts: none -> 1.35 us  [shards(): return (both[0], both[1])]
    pallas_call x1, Pallas kernels: 15.9 us -> 17 us  [shards(): pl.pallas_call(functools.partial(kernel, wide, freq), out_shape=result, i...]
where the time goes in v2:
time: 19.2 us; the launch traced here: 19 us
  Pallas kernels  17 us (89%)
  local copies, waits for them, and re-layouts  1.35 us (7%)
  between operations  0.64 us (3%)
    pallas_call x1, Pallas kernels, shards(): pl.pallas_call(functools.partial(kernel, wide, freq), out_shape=result, i...  17 us
    squeeze x1, local copies, waits for them, and re-layouts, shards(): return (both[0], both[1])  1.35 us

profile of v2, /device:TPU:0, one launch (start us, length us, event | category | flops | bytes accessed | tf_op | source)
XLA Modules:
  0.0 19.0 jit_solution(13618268699261122510)
XLA Ops:
  0.6 17.0 %shard_map.59 = f32[2,2,4,2,192]{4,3,2,1,0:T(2,128)} custom-call(s32[8]{0:T(128)} %orders_hbm.1, f32[2,4,192,512]{3,2,1,0:T(8,128)} %bitcast.6, bf16[2,4,2,192,768]{4,3,2,1,0:T(8,128)(2,1)} %beams_hbm.1, f32[5,4,768]{2,1,0:T(4,128)} %bitcast.7), custom_call_target="tpu_custom_call" | custom-call | tf_op jit(solution)/shard_map/pallas_call | solution.py:192
  17.7 1.3 %slice_bitcast_fusion = (f32[2,4,2,192]{3,2,1,0:T(2,128)}, f32[2,4,2,192]{3,2,1,0:T(2,128)}) fusion(f32[2,2,4,2,192]{4,3,2,1,0:T(2,128)} %shard_map.59), kind=kLoop, calls=%fused_computation | loop fusion | bytes 49152 | tf_op jit(solution)/shard_map/squeeze | solution.py:224

commit v3 on v2

--- a/solution.py
+++ b/solution.py
@@ -10,8 +10,8 @@
 
 TIME = 2048
 QUARTER = TIME // 4
+SHIFT = QUARTER.bit_length() - 1
 BAND = 4
-PIECES = 2
 MESH = pl.DeviceIdType.MESH
 NT = (((1,), (1,)), ((), ()))
 NN = (((1,), (0,)), ((), ()))
@@ -19,7 +19,7 @@
 
 def cosine(steps):
     near = steps + QUARTER // 2
-    quadrant = (near // QUARTER) & 3
+    quadrant = (near >> SHIFT) & 3
     x = ((near & (QUARTER - 1)) - QUARTER // 2).astype(jnp.float32) * (2.0 * math.pi / TIME)
     y = x * x
     cos = 1.0 + y * (-1 / 2 + y * (1 / 24 + y * (-1 / 720 + y * (1 / 40320))))
@@ -83,7 +83,7 @@
     order_copy.wait()
     order = jnp.zeros(shape, jnp.int32)
     for i in range(total):
-        order = jnp.where(row // 2 == i, orders[i], order)
+        order = jnp.where(row >> 1 == i, orders[i], order)
     steps = order * time
     imag_row = (row & 1) == 1
     factor = 1.0 / math.sqrt(TIME)
@@ -122,9 +122,8 @@
     for copy in sends:
         copy.wait_recv()
 
-    order_of_row = lax.broadcasted_iota(jnp.int32, (rows, modes), 0) // 2
+    order_of_row = lax.broadcasted_iota(jnp.int32, (rows, modes), 0) >> 1
     targets = [{"pol": 1 - my_pol}, {"freq": before}, {"freq": before, "pol": 1 - my_pol}]
-    piece = blocks // PIECES
     proj_sends = []
     for f in range(blocks):
         summed = part[my_wide, f]
@@ -143,27 +142,24 @@
                     left, beams[o, f, c], NN, preferred_element_type=jnp.float32
                 )
         proj[f] = acc
-        if f % piece == piece - 1:
-            g = f // piece
-            span = pl.ds(g * piece, piece)
-            for s, target in enumerate(targets):
-                copy = pltpu.make_async_remote_copy(
-                    src_ref=proj.at[span],
-                    dst_ref=recv_proj.at[s, span],
-                    send_sem=psend_sem.at[s, g],
-                    recv_sem=precv_sem.at[s, g],
-                    device_id=target,
-                    device_id_type=MESH,
-                )
-                copy.start()
-                proj_sends.append(copy)
+        for s, target in enumerate(targets):
+            copy = pltpu.make_async_remote_copy(
+                src_ref=proj.at[f],
+                dst_ref=recv_proj.at[s, f],
+                send_sem=psend_sem.at[s, f],
+                recv_sem=precv_sem.at[s, f],
+                device_id=target,
+                device_id_type=MESH,
+            )
+            copy.start()
+            proj_sends.append(copy)
     spectra_copy.wait()
     for copy in proj_sends:
         copy.wait_recv()
 
     extended = [proj[f] + recv_proj[0, f] for f in range(blocks)]
     extended += [recv_proj[1, f] + recv_proj[2, f] for f in range(blocks)]
-    order_of_row = lax.broadcasted_iota(jnp.int32, (rows, beams.shape[-1]), 0) // 2
+    order_of_row = lax.broadcasted_iota(jnp.int32, (rows, beams.shape[-1]), 0) >> 1
     for f in range(blocks):
         mixed = spectra[0, f : f + 1] * extended[f]
         for d in range(1, BAND + 1):
@@ -209,17 +205,22 @@
             dma,
             dma((wide - 1,)),
             dma((wide - 1,)),
-            dma((3, PIECES)),
-            dma((3, PIECES)),
+            dma((3, blocks)),
+            dma((3, blocks)),
         ],
         compiler_params=pltpu.CompilerParams(
-            collective_id=0, has_side_effects=True, vmem_limit_bytes=64 << 20
+            collective_id=0, has_side_effects=True, vmem_limit_bytes=48 << 20
         ),
     )(
-        m_orders,
-        jnp.transpose(visibilities, (0, 2, 3, 1)),
-        beams,
-        jnp.transpose(spectra, (1, 0, 2)),
+        *(
+            pltpu.with_memory_space_constraint(array, pltpu.HBM)
+            for array in (
+                m_orders,
+                jnp.transpose(visibilities, (0, 2, 3, 1)),
+                beams,
+                jnp.transpose(spectra, (1, 0, 2)),
+            )
+        )
     )
     return both[0], both[1]
 

time: 19.2 us -> 17.8 us (0.927)
  local copies, waits for them, and re-layouts: 1.35 us -> 0.61 us
  Pallas kernels: 17 us -> 16.4 us
    squeeze x1, local copies, waits for them, and re-layouts: 1.35 us -> 0.61 us  [shards(): return (both[0], both[1])]
    pallas_call x1, Pallas kernels: 17 us -> 16.4 us  [shards(): pl.pallas_call(functools.partial(kernel, wide, freq), out_shape=result, i...]
where the time goes in v3:
time: 17.8 us; the launch traced here: 17.6 us
  Pallas kernels  16.4 us (92%)
  between operations  0.64 us (4%)
  local copies, waits for them, and re-layouts  0.61 us (3%)
    pallas_call x1, Pallas kernels, shards(): pl.pallas_call(functools.partial(kernel, wide, freq), out_shape=result, i...  16.4 us
    squeeze x1, local copies, waits for them, and re-layouts, shards(): return (both[0], both[1])  0.61 us

profile of v3, /device:TPU:0, one launch (start us, length us, event | category | flops | bytes accessed | tf_op | source)
XLA Modules:
  0.0 17.6 jit_solution(10591726923763438583)
XLA Ops:
  0.6 16.4 %shard_map.59 = f32[2,2,4,2,192]{4,3,2,1,0:T(2,128)S(1)} custom-call(s32[8]{0:T(128)} %orders_hbm.1, f32[2,4,192,512]{3,2,1,0:T(8,128)} %bitcast.6, bf16[2,4,2,192,768]{4,3,2,1,0:T(8,128)(2,1)} %beams_hbm.1, f32[5,4,768]{2,1,0:T(4,128)} %bitcast.7), custom_call_target="tpu_custom_call" | custom-call | tf_op jit(solution)/shard_map/pallas_call | solution.py:188
  17.0 0.6 %slice_bitcast_fusion = (f32[2,4,2,192]{3,2,1,0:T(2,128)}, f32[2,4,2,192]{3,2,1,0:T(2,128)}) fusion(f32[2,2,4,2,192]{4,3,2,1,0:T(2,128)S(1)} %shard_map.59), kind=kLoop, calls=%fused_computation | loop fusion | bytes 49152 | tf_op jit(solution)/shard_map/squeeze | solution.py:225

commit v4 on v3

--- a/solution.py
+++ b/solution.py
@@ -72,8 +72,6 @@
         pltpu.make_async_copy(beams_hbm.at[:, f], beams.at[:, f], beam_sem.at[f])
         for f in range(blocks)
     ]
-    for copy in beam_copies:
-        copy.start()
     spectra_copy = pltpu.make_async_copy(spectra_hbm, spectra, spectra_sem)
     spectra_copy.start()
 
@@ -95,6 +93,9 @@
 
     for f in range(blocks):
         vis_copies[f].wait()
+        if f == blocks - 1:
+            for copy in beam_copies:
+                copy.start()
         both = jnp.zeros((4 * total, modes), jnp.float32)
         small = jnp.zeros((2 * total, modes), jnp.float32)
         for c in range(2):
@@ -123,7 +124,7 @@
         copy.wait_recv()
 
     order_of_row = lax.broadcasted_iota(jnp.int32, (rows, modes), 0) >> 1
-    targets = [{"pol": 1 - my_pol}, {"freq": before}, {"freq": before, "pol": 1 - my_pol}]
+    targets = [{"freq": before}, {"freq": before, "pol": 1 - my_pol}, {"pol": 1 - my_pol}]
     proj_sends = []
     for f in range(blocks):
         summed = part[my_wide, f]
@@ -154,13 +155,15 @@
             copy.start()
             proj_sends.append(copy)
     spectra_copy.wait()
-    for copy in proj_sends:
-        copy.wait_recv()
-
-    extended = [proj[f] + recv_proj[0, f] for f in range(blocks)]
-    extended += [recv_proj[1, f] + recv_proj[2, f] for f in range(blocks)]
+    extended = []
+    for f in range(blocks):
+        proj_sends[3 * f + 2].wait_recv()
+        extended.append(proj[f] + recv_proj[2, f])
     order_of_row = lax.broadcasted_iota(jnp.int32, (rows, beams.shape[-1]), 0) >> 1
     for f in range(blocks):
+        proj_sends[3 * f].wait_recv()
+        proj_sends[3 * f + 1].wait_recv()
+        extended.append(recv_proj[0, f] + recv_proj[1, f])
         mixed = spectra[0, f : f + 1] * extended[f]
         for d in range(1, BAND + 1):
             mixed = mixed + spectra[d, f : f + 1] * extended[f + d]

time: 17.8 us -> 18.1 us (1.017)
  Pallas kernels: 16.4 us -> 16.7 us
    pallas_call x1, Pallas kernels: 16.4 us -> 16.7 us  [shards(): pl.pallas_call(functools.partial(kernel, wide, freq), out_shape=result, i...]
where the time goes in v4:
time: 18.1 us; the launch traced here: 17.9 us
  Pallas kernels  16.7 us (92%)
  between operations  0.64 us (4%)
  local copies, waits for them, and re-layouts  0.61 us (3%)
    pallas_call x1, Pallas kernels, shards(): pl.pallas_call(functools.partial(kernel, wide, freq), out_shape=result, i...  16.7 us
    squeeze x1, local copies, waits for them, and re-layouts, shards(): return (both[0], both[1])  0.61 us

profile of v4, /device:TPU:0, one launch (start us, length us, event | category | flops | bytes accessed | tf_op | source)
XLA Modules:
  0.0 17.9 jit_solution(6717785144229032898)
XLA Ops:
  0.6 16.7 %shard_map.59 = f32[2,2,4,2,192]{4,3,2,1,0:T(2,128)S(1)} custom-call(s32[8]{0:T(128)} %orders_hbm.1, f32[2,4,192,512]{3,2,1,0:T(8,128)} %bitcast.6, bf16[2,4,2,192,768]{4,3,2,1,0:T(8,128)(2,1)} %beams_hbm.1, f32[5,4,768]{2,1,0:T(4,128)} %bitcast.7), custom_call_target="tpu_custom_call" | custom-call | tf_op jit(solution)/shard_map/pallas_call | solution.py:191
  17.3 0.6 %slice_bitcast_fusion = (f32[2,4,2,192]{3,2,1,0:T(2,128)}, f32[2,4,2,192]{3,2,1,0:T(2,128)}) fusion(f32[2,2,4,2,192]{4,3,2,1,0:T(2,128)S(1)} %shard_map.59), kind=kLoop, calls=%fused_computation | loop fusion | bytes 49152 | tf_op jit(solution)/shard_map/squeeze | solution.py:228

commit v5 on v4

--- a/solution.py
+++ b/solution.py
@@ -72,6 +72,8 @@
         pltpu.make_async_copy(beams_hbm.at[:, f], beams.at[:, f], beam_sem.at[f])
         for f in range(blocks)
     ]
+    for copy in beam_copies:
+        copy.start()
     spectra_copy = pltpu.make_async_copy(spectra_hbm, spectra, spectra_sem)
     spectra_copy.start()
 
@@ -93,9 +95,6 @@
 
     for f in range(blocks):
         vis_copies[f].wait()
-        if f == blocks - 1:
-            for copy in beam_copies:
-                copy.start()
         both = jnp.zeros((4 * total, modes), jnp.float32)
         small = jnp.zeros((2 * total, modes), jnp.float32)
         for c in range(2):
@@ -161,9 +160,12 @@
         extended.append(proj[f] + recv_proj[2, f])
     order_of_row = lax.broadcasted_iota(jnp.int32, (rows, beams.shape[-1]), 0) >> 1
     for f in range(blocks):
-        proj_sends[3 * f].wait_recv()
-        proj_sends[3 * f + 1].wait_recv()
-        extended.append(recv_proj[0, f] + recv_proj[1, f])
+        if f in (0, blocks - 1):
+            arriving = range(blocks - 1) if f == 0 else range(blocks - 1, blocks)
+            for g in arriving:
+                proj_sends[3 * g].wait_recv()
+                proj_sends[3 * g + 1].wait_recv()
+            extended += [recv_proj[0, g] + recv_proj[1, g] for g in arriving]
         mixed = spectra[0, f : f + 1] * extended[f]
         for d in range(1, BAND + 1):
             mixed = mixed + spectra[d, f : f + 1] * extended[f + d]

time: 18.1 us -> 18.1 us (level)
  no operation moved by 1% of the time
where the time goes in v5:
time: 18.1 us; the launch traced here: 17.9 us
  Pallas kernels  16.7 us (92%)
  between operations  0.64 us (4%)
  local copies, waits for them, and re-layouts  0.61 us (3%)
    pallas_call x1, Pallas kernels, shards(): pl.pallas_call(functools.partial(kernel, wide, freq), out_shape=result, i...  16.7 us
    squeeze x1, local copies, waits for them, and re-layouts, shards(): return (both[0], both[1])  0.61 us

profile of v5, /device:TPU:0, one launch (start us, length us, event | category | flops | bytes accessed | tf_op | source)
XLA Modules:
  0.0 17.9 jit_solution(4728836902680244682)
XLA Ops:
  0.6 16.7 %shard_map.59 = f32[2,2,4,2,192]{4,3,2,1,0:T(2,128)S(1)} custom-call(s32[8]{0:T(128)} %orders_hbm.1, f32[2,4,192,512]{3,2,1,0:T(8,128)} %bitcast.6, bf16[2,4,2,192,768]{4,3,2,1,0:T(8,128)(2,1)} %beams_hbm.1, f32[5,4,768]{2,1,0:T(4,128)} %bitcast.7), custom_call_target="tpu_custom_call" | custom-call | tf_op jit(solution)/shard_map/pallas_call | solution.py:193
  17.3 0.6 %slice_bitcast_fusion = (f32[2,4,2,192]{3,2,1,0:T(2,128)}, f32[2,4,2,192]{3,2,1,0:T(2,128)}) fusion(f32[2,2,4,2,192]{4,3,2,1,0:T(2,128)S(1)} %shard_map.59), kind=kLoop, calls=%fused_computation | loop fusion | bytes 49152 | tf_op jit(solution)/shard_map/squeeze | solution.py:230
